TPU v7x, 512 devices: a whole 4x4x16 slice. The times are simulated.
512 devices in a mesh: grp: 16 (over y, z_hi), sp: 32 (over z_lo, x, core).
Axes of the slice: x: 4, y: 4, z: 16 (z_hi: 4, z_lo: 4; z = z_hi * 4 + z_lo), core: 2. Of those that a mesh axis runs over, the one named last changes fastest.
Arguments:
- queries: bfloat16 [16, 2048, 4096], P('grp', 'sp'), may hold values from -180 to 180
- keys: bfloat16 [16, 2048, 4096], P('grp', 'sp'), may hold values from -7 to 7
- values: bfloat16 [16, 2048, 4096], P('grp', 'sp'), may hold values from -6 to 6
- positions: int32 [16, 2048], P('grp'), may hold values from 0 to 2047, each once within a row
- anchor: int32 [1], replicated, may hold values from 0 to 1048575
Outputs:
- attended: bfloat16 [16, 2048, 4096], P('grp', 'sp')
Inputs may be any that keep to these rules, and one draw needn't show every extreme that they name: Each group's row of positions holds every number of 0 to 2047 once.
All inputs are finite; a program needn't handle non-finite values.
Results may differ from a plain program's by a relative error of at most 0.0048.
Values may be sent and summed in bfloat16 or wider, within the bound.
A program may use at most 64 MiB of HBM per device.

v0:
```python
import math

import jax
import jax.numpy as jnp
from jax import lax
from jax.sharding import PartitionSpec as P

HD = 128


NEG = -1e30


def broadcast(block, axis, source):
    block = jnp.where(lax.axis_index(axis) == source, block, jnp.zeros_like(block))
    return lax.psum(block, axis)


def attend(q_heads, k_heads, v_heads, ak_heads, av_heads, order, skip_anchor):
    length, width = q_heads.shape
    head_count = width // HD
    block_rows = min(512, length)
    block_count = length // block_rows
    score_scale = 1.0 / math.sqrt(HD)
    key_rows = jnp.concatenate([k_heads, ak_heads], 0).reshape(2 * length, head_count, HD)
    value_rows = jnp.concatenate([v_heads, av_heads], 0).reshape(2 * length, head_count, HD)
    query_blocks = q_heads.reshape(block_count, block_rows, head_count, HD)
    order_blocks = order.reshape(block_count, block_rows)

    def one_block(pieces):
        query_block, query_order = pieces
        scores = (
            jnp.einsum("qhd,khd->hqk", query_block, key_rows, preferred_element_type=jnp.float32)
            * score_scale
        )
        visible = order[None, :] <= query_order[:, None]
        local_part = jnp.where(visible[None], scores[:, :, :length], NEG)
        far_part = jnp.where(skip_anchor, NEG, scores[:, :, length:])
        joined = jnp.concatenate([local_part, far_part], 2)
        top_score = jnp.max(joined, axis=2, keepdims=True)
        expo = jnp.exp(joined - top_score)
        probs = (expo / jnp.sum(expo, axis=2, keepdims=True)).astype(jnp.bfloat16)
        output = jnp.einsum("hqk,khd->qhd", probs, value_rows, preferred_element_type=jnp.float32)
        return output.astype(jnp.bfloat16).reshape(block_rows, width)

    return lax.map(one_block, (query_blocks, order_blocks)).reshape(length, width)


def on_device(queries, keys, values, positions, anchor):
    group_count = lax.axis_size("grp")
    anchor_root = anchor[0] % group_count
    group_index = lax.axis_index("grp")
    q_heads, k_heads, v_heads = (
        lax.all_to_all(queries, "sp", split_axis=2, concat_axis=1, tiled=True),
        lax.all_to_all(keys, "sp", split_axis=2, concat_axis=1, tiled=True),
        lax.all_to_all(values, "sp", split_axis=2, concat_axis=1, tiled=True),
    )
    ak_heads, av_heads = (
        broadcast(k_heads, "grp", anchor_root),
        broadcast(v_heads, "grp", anchor_root),
    )
    attended_heads = attend(
        q_heads[0],
        k_heads[0],
        v_heads[0],
        ak_heads[0],
        av_heads[0],
        positions[0],
        group_index == anchor_root,
    )
    restored = lax.all_to_all(attended_heads[None], "sp", split_axis=1, concat_axis=2, tiled=True)
    return restored


def solution(mesh):
    return jax.shard_map(
        on_device,
        mesh=mesh,
        in_specs=(
            P("grp", "sp", None),
            P("grp", "sp", None),
            P("grp", "sp", None),
            P("grp", None),
            P(),
        ),
        out_specs=P("grp", "sp", None),
        check_vma=False,
    )
```

profile of v0, /device:TPU:1, one launch (start us, length us, event | category | flops | bytes accessed | tf_op | source)
XLA Modules:
  0.0 426.6 jit_solution(17305537959684867743)
XLA Ops:
  6.5 4.9 %copy.39 = bf16[1,64,4096]{1,0,2:T(2,128)(2,1)S(1)} copy(bf16[1,64,4096]{2,1,0:T(8,128)(2,1)} %param.8) | data formatting | bytes 1048576 | tf_op args[1]
  11.9 22.3 %reduce.11 = bf16[4096,64]{1,0:T(8,128)(2,1)S(1)} reduce(bf16[4096,1,64]{2,1,0:T(2,128)(2,1)S(1)} %bitcast.125, bf16[]{:T(256)} %broadcast.142), dimensions={1}, to_apply=%bitcast.84.reduce_sub_computation | reduce | bytes 1048578
  35.7 11.0 %all-to-all-start.1 = ((bf16[32,2,4096]{2,1,0:T(2,128)(2,1)}), bf16[32,2,4096]{2,1,0:T(2,128)(2,1)}, u32[]{:S(2)}, u32[]{:S(2)}) async-start(bf16[32,2,4096]{2,1,0:T(2,128)(2,1)} %reshape.307), calls=%async_computation.1 | async-start | bytes 1048576 | tf_op jit(solution)/shard_map/all_to_all | solution.py:55
  46.8 4.9 %copy.43 = bf16[1,64,4096]{1,0,2:T(2,128)(2,1)S(1)} copy(bf16[1,64,4096]{2,1,0:T(8,128)(2,1)} %param.9) | data formatting | bytes 1048576 | tf_op args[2]
  51.7 22.3 %reduce.10 = bf16[4096,64]{1,0:T(8,128)(2,1)S(1)} reduce(bf16[4096,1,64]{2,1,0:T(2,128)(2,1)S(1)} %bitcast.126, bf16[]{:T(256)} %broadcast.142), dimensions={1}, to_apply=%bitcast.86.reduce_sub_computation | reduce | bytes 1048578
  75.5 7.9 %all-to-all-start.2 = ((bf16[32,2,4096]{2,1,0:T(2,128)(2,1)}), bf16[32,2,4096]{2,1,0:T(2,128)(2,1)}, u32[]{:S(2)}, u32[]{:S(2)}) async-start(bf16[32,2,4096]{2,1,0:T(2,128)(2,1)} %reshape.309), calls=%async_computation.2 | async-start | bytes 1048576 | tf_op jit(solution)/shard_map/all_to_all | solution.py:56
  83.4 4.9 %copy.36 = bf16[1,64,4096]{1,0,2:T(2,128)(2,1)S(1)} copy(bf16[1,64,4096]{2,1,0:T(8,128)(2,1)} %param.7) | data formatting | bytes 1048576 | tf_op args[0]
  88.3 22.3 %reduce.9 = bf16[4096,64]{1,0:T(8,128)(2,1)S(1)} reduce(bf16[4096,1,64]{2,1,0:T(2,128)(2,1)S(1)} %bitcast.127, bf16[]{:T(256)} %broadcast.142), dimensions={1}, to_apply=%bitcast.82.reduce_sub_computation | reduce | bytes 1048578
  112.2 7.7 %all-to-all-start = ((bf16[32,2,4096]{2,1,0:T(2,128)(2,1)}), bf16[32,2,4096]{2,1,0:T(2,128)(2,1)S(1)}, u32[]{:S(2)}, u32[]{:S(2)}) async-start(bf16[32,2,4096]{2,1,0:T(2,128)(2,1)} %reshape.305), calls=%async_computation | async-start | bytes 1048576 | tf_op jit(solution)/shard_map/all_to_all | solution.py:54
  120.9 4.1 reshape.308
  125.0 2.3 copy.40
  127.4 4.1 reshape.310
  131.6 3.6 copy.44
  142.2 2.3 copy.37
  144.8 201.7 %all-reduce.3.cloned.1.call-done = (bf16[2048,128]{1,0:T(8,128)(2,1)}, bf16[2048,128]{1,0:T(8,128)(2,1)}) async-done(((bf16[2048,128]{1,0:T(8,128)(2,1)}, bf16[2048,128]{1,0:T(8,128)(2,1)}), (bf16[2048,128]{1,0:T(8,128)(2,1)}, bf16[2048,128]{1,0:T(8,128)(2,1)})) %all-reduce.3.cloned.1.call-update) | async-done | bytes 1048592 | tf_op jit(solution)/shard_map/psum | solution.py:16
  346.5 2.1 maximum_bitcast_fusion.1
  349.7 26.6 %while.10 = (s32[]{:T(128)}, bf16[4,512,128]{2,1,0:T(8,128)(2,1)}, s32[1,2048]{1,0:T(1,128)S(1)}, s32[4,512]{1,0:T(4,128)S(1)}, bf16[4,512,1,128]{3,1,2,0:T(8,12...) while((s32[]{:T(128)}, bf16[4,512,128]{2,1,0:T(8,128)(2,1)}, ...), condition=%wide.region_6.7_spmd, body=%wide.region_2.6_spmd.sunk | while | flops 1095826432 | bytes 48530048 | solution.py:46
  353.7 2.7 fusion.38
  360.4 2.7 fusion.38
  367.0 2.7 fusion.38
  373.7 2.7 fusion.38
  376.3 1.8 copy.58
  378.1 11.4 %reduce.12 = bf16[2048,128]{1,0:T(8,128)(2,1)S(1)} reduce(bf16[2048,1,128]{2,1,0:T(2,128)(2,1)S(1)} %bitcast.133, bf16[]{:T(256)} %broadcast.142), dimensions={1}, to_apply=%bitcast.92.reduce_sub_computation | reduce | bytes 1048578
  389.7 28.6 %all_to_all.63 = bf16[32,2,4096]{2,1,0:T(2,128)(2,1)S(1)} all-to-all(bf16[32,2,4096]{2,1,0:T(2,128)(2,1)S(1)} %reshape.311), channel_id=1, replica_groups=mesh['grp'=16,'sp'=32] {'sp'}, dimensions={0} | all-to-all | bytes 1048576 | tf_op jit(solution)/shard_map/all_to_all | solution.py:71
  (63 shorter events, 31.3 us)
Async XLA Ops:
  35.7 39.8 %all-to-all-start.1 = ((bf16[32,2,4096]{2,1,0:T(2,128)(2,1)}), bf16[32,2,4096]{2,1,0:T(2,128)(2,1)}, u32[]{:S(2)}, u32[]{:S(2)}) async-start(bf16[32,2,4096]{2,1,0:T(2,128)(2,1)} %reshape.307), calls=%async_computation.1 | async-start | bytes 1048576 | tf_op jit(solution)/shard_map/all_to_all | solution.py:55
  75.5 36.6 %all-to-all-start.2 = ((bf16[32,2,4096]{2,1,0:T(2,128)(2,1)}), bf16[32,2,4096]{2,1,0:T(2,128)(2,1)}, u32[]{:S(2)}, u32[]{:S(2)}) async-start(bf16[32,2,4096]{2,1,0:T(2,128)(2,1)} %reshape.309), calls=%async_computation.2 | async-start | bytes 1048576 | tf_op jit(solution)/shard_map/all_to_all | solution.py:56
  112.2 28.8 %all-to-all-start = ((bf16[32,2,4096]{2,1,0:T(2,128)(2,1)}), bf16[32,2,4096]{2,1,0:T(2,128)(2,1)S(1)}, u32[]{:S(2)}, u32[]{:S(2)}) async-start(bf16[32,2,4096]{2,1,0:T(2,128)(2,1)} %reshape.305), calls=%async_computation | async-start | bytes 1048576 | tf_op jit(solution)/shard_map/all_to_all | solution.py:54
  119.9 226.6 %all-reduce.3.cloned.1.call-start = ((), (), s32[]{:S(2)}) async-start(), calls=%async_computation.4 | async-start | bytes 2097152 | tf_op jit(solution)/shard_map/psum | solution.py:16
  131.6 7.4 %copy-start.2 = (s32[1,2048]{1,0:T(1,128)S(1)}, s32[1,2048]{1,0:T(1,128)}, u32[]{:S(2)}) copy-start(s32[1,2048]{1,0:T(1,128)} %param.10) | copy-start | bytes 24580
  144.5 204.1 %copy-start = (bf16[1,32,64,128]{3,2,1,0:T(8,128)(2,1)S(1)}, bf16[1,32,64,128]{3,2,1,0:T(8,128)(2,1)}, u32[]{:S(2)}) copy-start(bf16[1,32,64,128]{3,2,1,0:T(8,128)(2,1)} %copy.41) | copy-start | bytes 1572868
  352.2 1.5 copy-start.1
  358.9 1.5 copy-start.1
  365.5 1.5 copy-start.1
  372.2 1.5 copy-start.1
Sparse Core Ops, SparseCore 0:
  138.6 207.9 all-reduce.2
where the time goes:
time: 428 us; the launch traced here: 427 us
  waiting for transfers between devices  202 us (47%)
  other arithmetic  93 us (22%)
  local copies, waits for them, and re-layouts  46.2 us (11%)
  blocking collectives  28.6 us (7%)
  starting transfers between devices  27 us (6%)
  matrix products  15.6 us (4%)
  between operations  14.3 us (3%)
    psum x1, waiting for transfers between devices, broadcast(): return lax.psum(block, axis)  202 us
    unnamed x5, other arithmetic  79 us
    unnamed x21, local copies, waits for them, and re-layouts  31.8 us
    all_to_all x1, blocking collectives, on_device(): lax.all_to_all(attended_heads[None], 'sp', split_axis=1, concat_axis=2, t...  28.6 us
    all_to_all x1, starting transfers between devices, on_device(): lax.all_to_all(keys, 'sp', split_axis=2, concat_axis=1, tiled=True)  11 us
    dot_general x4, matrix products, one_block(): jnp.einsum('hqk,khd->qhd', probs, value_rows, preferred_element_type=jnp....  10.6 us
  transfers between devices with their start and end apart: 4, of which 1 were waited for; matrix products, arithmetic and copies ran while one was open for 19% of the time, Pallas kernels for 0%

commit v1 on v0

v1 whole, which is shorter than its diff:
```python
import functools
import math

import jax
import jax.numpy as jnp
from jax import lax
from jax.experimental import pallas as pl
from jax.experimental.pallas import tpu as pltpu
from jax.sharding import PartitionSpec as P

HD = 128
NEG = -1e30
NY = 4
NZ = 4
HALVES = 2
C = math.log2(math.e) / math.sqrt(HD)
MESH = pl.DeviceIdType.MESH
NT = (((1,), (1,)), ((), ()))


def scores_of(q, keys):
    return lax.dot_general(q, keys, NT, preferred_element_type=jnp.float32)


def weigh(s_scr, m, values, length):
    parts = [
        jnp.exp2(s_scr[:, j : j + 128] - m).astype(jnp.bfloat16)
        for j in range(0, length, 128)
    ]
    p = jnp.concatenate(parts, axis=1)
    wide = jnp.concatenate([values, jnp.ones_like(values)], axis=1)
    return jnp.dot(p, wide, preferred_element_type=jnp.float32)


def row_max(mx):
    return jnp.broadcast_to(jnp.max(mx, axis=1, keepdims=True), mx.shape)


def local_block(r0, bq, length, qh, kh, vh, posc, posr, s_scr, acc_loc, m_loc, l_loc):
    rows = pl.ds(r0, bq)
    s = scores_of(qh[rows, :], kh[...])
    mine = posc[rows, :]
    mx = jnp.full((bq, 128), NEG, jnp.float32)
    for j in range(0, length, 128):
        piece = jnp.where(mine >= posr[:, j : j + 128], s[:, j : j + 128] * C, NEG)
        s_scr[:, j : j + 128] = piece
        mx = jnp.maximum(mx, piece)
    m = row_max(mx)
    acc = weigh(s_scr, m, vh[...], length)
    acc_loc[rows, :] = acc[:, :HD]
    l_loc[rows, :] = acc[:, HD:]
    m_loc[rows, :] = m


def far_block(r0, bq, length, bias, qh, ak, av, s_scr, acc_loc, m_loc, l_loc, oh):
    rows = pl.ds(r0, bq)
    s = scores_of(qh[rows, :], ak[...])
    mx = jnp.full((bq, 128), NEG, jnp.float32)
    for j in range(0, length, 128):
        piece = s[:, j : j + 128] * C
        s_scr[:, j : j + 128] = piece
        mx = jnp.maximum(mx, piece)
    m_far = row_max(mx)
    acc = weigh(s_scr, m_far, av[...], length)
    m_far = m_far + bias
    m = jnp.maximum(m_loc[rows, :], m_far)
    w_loc = jnp.exp2(m_loc[rows, :] - m)
    w_far = jnp.exp2(m_far - m)
    top = acc_loc[rows, :] * w_loc + acc[:, :HD] * w_far
    bottom = l_loc[rows, :] * w_loc + acc[:, HD:] * w_far
    oh[rows, :] = (top / bottom).astype(jnp.bfloat16)


def kernel(
    shards, length, tokens, bq,
    anchor_ref, pos_ref, q_ref, k_ref, v_ref, out_ref,
    qh, kh, vh, ak, av, oh, posc, posr, s_scr, acc_loc, m_loc, l_loc,
    ybuf, abuf, bbuf,
    flat_send, flat_recv, y_send, y_recv, a_send, a_recv, b_send, b_recv, g_send, g_recv,
):
    grp = lax.axis_index("grp")
    me = lax.axis_index("sp")
    y = grp // NZ
    z = grp % NZ
    quarter = length // NY
    part = quarter // HALVES
    blocks = length // bq
    per_block = bq // tokens

    def pair_a(zz):
        return zz + 1 - 2 * (zz % 2)

    def pair_b(zz):
        return (zz + 3 + 2 * (zz % 2)) % NZ

    root = lax.rem(anchor_ref[0], NY * NZ)
    root_y = lax.div(root, NZ)
    root_z = lax.rem(root, NZ)
    pick_a = jnp.where(root_z == pair_a(z), 1, 0)
    pick_b = jnp.where((root_z == z) | (root_z == pair_a(z)), 0, 1)
    bias = jnp.where(root == grp, NEG, 0.0)

    barrier = pltpu.get_barrier_semaphore()

    def greet(d, carry):
        peer = lax.rem(me + d, shards)
        pl.semaphore_signal(barrier, inc=1, device_id=(grp, peer), device_id_type=MESH)
        return carry

    lax.fori_loop(1, shards, greet, 0)
    for d in range(1, NY):
        pl.semaphore_signal(
            barrier, inc=1, device_id=(((y + d) % NY) * NZ + z, me), device_id_type=MESH
        )
    for other in (pair_a(z), pair_b(z)):
        pl.semaphore_signal(
            barrier, inc=1, device_id=(y * NZ + other, me), device_id_type=MESH
        )

    posr[...] = pos_ref[...].astype(jnp.float32)
    for j in range(0, length, 128):
        square = jnp.broadcast_to(posr[:, j : j + 128], (128, 128))
        posc[j : j + 128, :] = square.T

    pl.semaphore_wait(barrier, shards - 1 + NY - 1 + 2)

    my_rows = pl.ds(pl.multiple_of(me * tokens, tokens), tokens)
    my_columns = pl.ds(pl.multiple_of(me * HD, HD), HD)

    def scatter(i, src, dst):
        pltpu.make_async_copy(
            src.at[0, :, my_columns], dst.at[my_rows, :], flat_recv.at[i]
        ).start()

        def body(n, carry):
            peer = lax.rem(me + lax.rem(n + shards // 4 - 1, shards - 1) + 1, shards)
            columns = pl.ds(pl.multiple_of(peer * HD, HD), HD)
            pltpu.make_async_remote_copy(
                src_ref=src.at[0, :, columns],
                dst_ref=dst.at[my_rows, :],
                send_sem=flat_send.at[i],
                recv_sem=flat_recv.at[i],
                device_id=(grp, peer),
                device_id_type=MESH,
            ).start()
            return carry

        lax.fori_loop(0, shards - 1, body, 0)

    def arrived(i, dst):
        pltpu.make_async_copy(dst, dst, flat_recv.at[i]).wait()

    def own_rows(j, h):
        return pl.ds(pl.multiple_of(j * quarter + h * part, part), part)

    def y_start(c, src):
        h = c % HALVES
        pltpu.make_async_copy(src.at[own_rows(y, h), :], ybuf[c].at[y], y_recv.at[c]).start()
        for d in range(1, NY):
            j = (y + d) % NY
            pltpu.make_async_remote_copy(
                src_ref=src.at[own_rows(j, h), :],
                dst_ref=ybuf[c].at[y],
                send_sem=y_send.at[c],
                recv_sem=y_recv.at[c],
                device_id=(j * NZ + z, me),
                device_id_type=MESH,
            ).start()

    def pair_copy(c, buf, send, recv, other):
        return pltpu.make_async_remote_copy(
            src_ref=buf[c].at[0],
            dst_ref=buf[c].at[1],
            send_sem=send.at[c],
            recv_sem=recv.at[c],
            device_id=(y * NZ + other, me),
            device_id_type=MESH,
        )

    def a_copy(c):
        return pair_copy(c, abuf, a_send, a_recv, pair_a(z))

    def b_copy(c):
        return pair_copy(c, bbuf, b_send, b_recv, pair_b(z))

    def a_start(c):
        pltpu.make_async_copy(ybuf[c], ybuf[c], y_recv.at[c]).wait()
        abuf[c][0] = ybuf[c][root_y]
        a_copy(c).start()

    def b_start(c):
        a_copy(c).wait_recv()
        bbuf[c][0] = abuf[c][pick_a]
        b_copy(c).start()

    def g_copies(c, dst):
        rows = own_rows(y, c % HALVES)
        return [
            pltpu.make_async_remote_copy(
                src_ref=dst.at[rows, :],
                dst_ref=dst.at[rows, :],
                send_sem=g_send.at[c],
                recv_sem=g_recv.at[c],
                device_id=(((y + d) % NY) * NZ + z, me),
                device_id_type=MESH,
            )
            for d in range(1, NY)
        ]

    def g_start(c, dst):
        b_copy(c).wait_recv()
        dst[own_rows(y, c % HALVES), :] = bbuf[c][pick_b]
        for copy in g_copies(c, dst):
            copy.start()

    def three(sem):
        view = ybuf[0].at[pl.ds(0, NY - 1)]
        pltpu.make_async_copy(view, view, sem).wait()

    parts = range(HALVES)
    first = [h for h in parts]
    second = [HALVES + h for h in parts]

    def block_row(i):
        turn = lax.rem(i + lax.div(me, per_block), blocks)
        return pl.multiple_of(turn * bq, bq)

    def local(low, high):
        def body(i, carry):
            local_block(
                block_row(i), bq, length, qh, kh, vh, posc, posr, s_scr, acc_loc, m_loc, l_loc
            )
            return carry

        lax.fori_loop(low, high, body, 0)

    scatter(0, k_ref, kh)
    scatter(1, v_ref, vh)
    arrived(0, kh)
    for c in first:
        y_start(c, kh)
    scatter(2, q_ref, qh)
    for c in first:
        a_start(c)
    arrived(1, vh)
    for c in second:
        y_start(c, vh)
    for c in first:
        b_start(c)
    for c in second:
        a_start(c)
    arrived(2, qh)
    step = max(1, blocks // 4)
    local(0, step)
    for c in first:
        g_start(c, ak)
    local(step, 2 * step)
    for c in second:
        b_start(c)
    local(2 * step, blocks)
    for c in second:
        g_start(c, av)
    for c in first + second:
        three(g_recv.at[c])

    def out_copies(i):
        turn = lax.rem(i + lax.div(me, per_block), blocks)
        for n in range(per_block):
            peer = turn * per_block + n
            rows = pl.ds(pl.multiple_of(peer * tokens, tokens), tokens)
            src = oh.at[rows, :]
            dst = out_ref.at[0, :, my_columns]

            @pl.when(peer == me)
            def _():
                pltpu.make_async_copy(src, dst, flat_recv.at[3]).start()

            @pl.when(peer != me)
            def _():
                pltpu.make_async_remote_copy(
                    src_ref=src,
                    dst_ref=dst,
                    send_sem=flat_send.at[3],
                    recv_sem=flat_recv.at[3],
                    device_id=(grp, peer),
                    device_id_type=MESH,
                ).start()

    def far(i, carry):
        far_block(
            block_row(i), bq, length, bias, qh, ak, av, s_scr, acc_loc, m_loc, l_loc, oh
        )
        out_copies(i)
        return carry

    lax.fori_loop(0, blocks, far, 0)

    most = pl.ds(0, (shards - 1) * tokens)
    for i, buf in enumerate((kh, vh, qh, oh)):
        pltpu.make_async_copy(buf.at[most, :], buf.at[most, :], flat_send.at[i]).wait()
    for c in first + second:
        three(y_send.at[c])
        a_copy(c).wait_send()
        b_copy(c).wait_send()
        three(g_send.at[c])
    pltpu.make_async_copy(out_ref, out_ref, flat_recv.at[3]).wait()


def solution(mesh):
    shards = mesh.shape["sp"]

    def on_device(queries, keys, values, positions, anchor):
        tokens = queries.shape[1]
        length = tokens * shards
        bq = max(tokens, min(256, length // 4))
        part = length // NY // HALVES
        chunks = 2 * HALVES
        bf16 = jnp.bfloat16
        head = pltpu.VMEM((length, HD), bf16)
        wide = pltpu.VMEM((length, HD), jnp.float32)
        dma = pltpu.SemaphoreType.DMA
        vmem = pl.BlockSpec(memory_space=pltpu.VMEM)
        return pl.pallas_call(
            functools.partial(kernel, shards, length, tokens, bq),
            out_shape=jax.ShapeDtypeStruct(queries.shape, bf16),
            in_specs=[pl.BlockSpec(memory_space=pltpu.SMEM), vmem, vmem, vmem, vmem],
            out_specs=vmem,
            scratch_shapes=[
                head, head, head, head, head, head,
                wide,
                pltpu.VMEM((1, length), jnp.float32),
                pltpu.VMEM((bq, length), jnp.float32),
                wide, wide, wide,
                [pltpu.VMEM((NY, part, HD), bf16)] * chunks,
                [pltpu.VMEM((2, part, HD), bf16)] * chunks,
                [pltpu.VMEM((2, part, HD), bf16)] * chunks,
                dma((4,)), dma((4,)),
                dma((chunks,)), dma((chunks,)),
                dma((chunks,)), dma((chunks,)),
                dma((chunks,)), dma((chunks,)),
                dma((chunks,)), dma((chunks,)),
            ],
            compiler_params=pltpu.CompilerParams(collective_id=0, has_side_effects=True),
            name="star_attention",
        )(anchor, positions, queries, keys, values)

    return jax.shard_map(
        on_device,
        mesh=mesh,
        in_specs=(
            P("grp", "sp", None),
            P("grp", "sp", None),
            P("grp", "sp", None),
            P("grp", None),
            P(),
        ),
        out_specs=P("grp", "sp", None),
        check_vma=False,
    )
```

time: 428 us -> 111 us (0.26)
  waiting for transfers between devices: 202 us -> 0 us
  Pallas kernels: 0 us -> 107 us
  other arithmetic: 93 us -> 0 us
  local copies, waits for them, and re-layouts: 46.2 us -> 1.87 us
  blocking collectives: 28.6 us -> 0 us
  starting transfers between devices: 27 us -> 0 us
  matrix products: 15.6 us -> 0 us
  between operations: 14.3 us -> 0.66 us
    psum x1 -> x0, waiting for transfers between devices: 202 us -> none  [broadcast(): return lax.psum(block, axis)]
    pallas_call x0 -> x1, Pallas kernels: none -> 107 us  [on_device(): pl.pallas_call(functools.partial(kernel, shards, length, tokens, bq), out...]
    unnamed x5 -> x0, other arithmetic: 79 us -> none
    unnamed x21 -> x1, local copies, waits for them, and re-layouts: 31.8 us -> 1.87 us
    all_to_all x1 -> x0, blocking collectives: 28.6 us -> none  [on_device(): lax.all_to_all(attended_heads[None], 'sp', split_axis=1, concat_axis=2, t...]
    all_to_all x3 -> x0, starting transfers between devices: 26.7 us -> none  [the longest x1 11 us: on_device(): lax.all_to_all(keys, 'sp', split_axis=2, concat_axis=1, tiled=True)]
    dot_general x8 -> x0, matrix products: 15.6 us -> none  [the longest x4 10.6 us: one_block(): jnp.einsum('hqk,khd->qhd', probs, value_rows, preferred_element_type=jnp....]
    all_to_all x10 -> x0, local copies, waits for them, and re-layouts: 10.6 us -> none  [the longest x3 3.84 us: on_device(): lax.all_to_all(values, 'sp', split_axis=2, concat_axis=1, tiled=True)]
  transfers between devices with their start and end apart: 4 -> 0, of which waited for: 1 -> 0; matrix products, arithmetic and copies ran while one was open for 19% -> 0% of each run, Pallas kernels for 0% -> 0%
where the time goes in v1:
time: 111 us; the launch traced here: 110 us
  Pallas kernels  107 us (96%)
  local copies, waits for them, and re-layouts  1.87 us (2%)
    pallas_call x1, Pallas kernels, on_device(): pl.pallas_call(functools.partial(kernel, shards, length, tokens, bq), out...  107 us

profile of v1, /device:TPU:1, one launch (start us, length us, event | category | flops | bytes accessed | tf_op | source)
XLA Modules:
  0.0 109.8 jit_solution(12098566159459949015)
XLA Ops:
  0.7 107.2 %star_attention.1 = bf16[1,64,4096]{2,1,0:T(8,128)(2,1)} custom-call(s32[1]{0:T(128)S(6)} %copy.7.anchor_ref, s32[1,2048]{1,0:T(1,128)} %pos_ref.1, bf16[1,64,4096]{2,1,0:T(8,128)(2,1)} %q_ref.1, bf16[1,64,4096]{2,1,0:T(8,128)(2,1)} %k_ref.1, bf16[1,64,4096]{2,1,0:T(8,128)(2,1)} %v_ref.1), custom_call_target="tpu_custom_call" | custom-call | tf_op jit(solution)/shard_map/star_attention/pallas_call | solution.py:323
  107.9 1.9 %copy.8 = bf16[1,64,4096]{2,1,0:T(8,128)(2,1)} copy(bf16[1,64,4096]{2,1,0:T(8,128)(2,1)} %star_attention.1) | data formatting | bytes 1048576

commit v2 on v0

v2 whole, which is shorter than its diff:
```python
import functools
import math

import jax
import jax.numpy as jnp
from jax import lax
from jax.experimental import pallas as pl
from jax.experimental.pallas import tpu as pltpu
from jax.sharding import PartitionSpec as P

HD = 128
NEG = -1e30
NY = 4
NZ = 4
HALVES = 2
NL = 4
BQ = 512
C = math.log2(math.e) / math.sqrt(HD)
MESH = pl.DeviceIdType.MESH
NT = (((1,), (1,)), ((), ()))


def scores_of(q, keys):
    return lax.dot_general(q, keys, NT, preferred_element_type=jnp.float32)


def chances(s_scr, m, length):
    parts = [
        jnp.exp2(s_scr[:, j : j + 128] - m).astype(jnp.bfloat16)
        for j in range(0, length, 128)
    ]
    return jnp.concatenate(parts, axis=1)


def weigh(p, values):
    wide = jnp.concatenate([values, jnp.ones_like(values)], axis=1)
    return jnp.dot(p, wide, preferred_element_type=jnp.float32)


def row_max(mx):
    return jnp.broadcast_to(jnp.max(mx, axis=1, keepdims=True), mx.shape)


def local_block(r0, bq, length, qh, kh, vh, posc, posr, s_scr, acc_loc, m_loc, l_loc):
    rows = pl.ds(r0, bq)
    s = scores_of(qh[rows, :], kh[...])
    mine = posc[rows, :]
    mx = jnp.full((bq, 128), NEG, jnp.float32)
    for j in range(0, length, 128):
        piece = jnp.where(mine >= posr[:, j : j + 128], s[:, j : j + 128] * C, NEG)
        s_scr[:, j : j + 128] = piece
        mx = jnp.maximum(mx, piece)
    m = row_max(mx)
    acc = weigh(chances(s_scr, m, length), vh[...])
    acc_loc[rows, :] = acc[:, :HD]
    l_loc[rows, :] = acc[:, HD:]
    m_loc[rows, :] = m


def far_chances(r0, bq, length, qh, ak, s_scr, p_far, m_far):
    rows = pl.ds(r0, bq)
    s = scores_of(qh[rows, :], ak[...])
    mx = jnp.full((bq, 128), NEG, jnp.float32)
    for j in range(0, length, 128):
        piece = s[:, j : j + 128] * C
        s_scr[:, j : j + 128] = piece
        mx = jnp.maximum(mx, piece)
    m = row_max(mx)
    p_far[rows, :] = chances(s_scr, m, length)
    m_far[rows, :] = m


def far_block(r0, bq, bias, av, p_far, m_far, acc_loc, m_loc, l_loc, oh):
    rows = pl.ds(r0, bq)
    acc = weigh(p_far[rows, :], av[...])
    other = m_far[rows, :] + bias
    m = jnp.maximum(m_loc[rows, :], other)
    w_loc = jnp.exp2(m_loc[rows, :] - m)
    w_far = jnp.exp2(other - m)
    top = acc_loc[rows, :] * w_loc + acc[:, :HD] * w_far
    bottom = l_loc[rows, :] * w_loc + acc[:, HD:] * w_far
    oh[rows, :] = (top / bottom).astype(jnp.bfloat16)


def kernel(
    source, shards, length, tokens, bq,
    anchor_ref, pos_ref, q_ref, k_ref, v_ref, out_ref,
    qh, kh, vh, ak, av, oh, posc, posr, s_scr, p_far, acc_loc, m_loc, l_loc, m_far,
    ybuf,
    send, recv, q_recv, y_send, y_recv, z_send, z_recv, g_send, g_recv,
):
    grp = lax.axis_index("grp")
    me = lax.axis_index("sp")
    y = grp // NZ
    z = grp % NZ
    side = shards // NL
    zl = me // side
    spot = me % side
    step = (z + NZ - source) % NZ
    quarter = length // NY
    part = quarter // HALVES
    stretch = length // NL
    per_stretch = stretch // bq
    per_block = bq // tokens

    def head_of(lane):
        return lane + (z % 2) * (NL - 1 - 2 * lane)

    def turned(lane, d):
        if d == 0:
            return lane
        if d == 1:
            return lane + 1 - 2 * (lane % 2)
        if d == 2:
            return (lane + 2) % NL
        return NL - 1 - lane

    opposite = (NL - 1 - zl) * side + spot
    above = (y * NZ + (z + 1) % NZ, opposite)
    below = (y * NZ + (z + NZ - 1) % NZ, opposite)
    near_top = (zl // 2 + step) % 2

    root = lax.rem(anchor_ref[0], NY * NZ)
    root_y = lax.div(root, NZ)
    bias = jnp.where(root == grp, NEG, 0.0)

    barrier = pltpu.get_barrier_semaphore()

    def greet(d, carry):
        peer = lax.rem(me + d, shards)
        pl.semaphore_signal(barrier, inc=1, device_id=(grp, peer), device_id_type=MESH)
        return carry

    y_peers = [(((y + d) % NY) * NZ + z, me) for d in range(1, NY)]
    for peer in y_peers + [above, below]:
        pl.semaphore_signal(barrier, inc=1, device_id=peer, device_id_type=MESH)
    lax.fori_loop(1, shards, greet, 0)

    posr[...] = pos_ref[...].astype(jnp.float32)
    for j in range(0, length, 128):
        square = jnp.broadcast_to(posr[:, j : j + 128], (128, 128))
        posc[j : j + 128, :] = square.T

    pl.semaphore_wait(barrier, shards - 1 + NY - 1 + 2)

    my_rows = pl.ds(pl.multiple_of(me * tokens, tokens), tokens)
    my_head = head_of(zl) * side + spot
    my_columns = pl.ds(pl.multiple_of(my_head * HD, HD), HD)

    def remote(src, dst, send_sem, recv_sem, peer):
        return pltpu.make_async_remote_copy(
            src_ref=src,
            dst_ref=dst,
            send_sem=send_sem,
            recv_sem=recv_sem,
            device_id=peer,
            device_id_type=MESH,
        )

    def scatter(i, src, dst, recv_sem, order):
        for d in order:
            lane = turned(zl, d)

            def body(n, carry, lane=lane):
                place = lax.rem(spot + n, side)
                head = head_of(lane) * side + place
                columns = pl.ds(pl.multiple_of(head * HD, HD), HD)
                remote(
                    src.at[0, :, columns], dst.at[my_rows, :], send.at[i], recv_sem,
                    (grp, lane * side + place),
                ).start()
                return carry

            if d == 0:
                pltpu.make_async_copy(
                    src.at[0, :, my_columns], dst.at[my_rows, :], recv_sem
                ).start()
            lax.fori_loop(1 if d == 0 else 0, side, body, 0)

    def arrived(dst, sem):
        pltpu.make_async_copy(dst, dst, sem).wait()

    def own_rows(j, c):
        start = j * quarter + (c % HALVES) * part
        return pl.ds(pl.multiple_of(start, part), part)

    def y_start(c, src):
        pltpu.make_async_copy(src.at[own_rows(y, c), :], ybuf[c].at[y], y_recv.at[c]).start()
        for d in range(1, NY):
            j = (y + d) % NY
            remote(
                src.at[own_rows(j, c), :], ybuf[c].at[y], y_send.at[c], y_recv.at[c],
                (j * NZ + z, me),
            ).start()

    def z_copy(c, dst, peer):
        rows = dst.at[own_rows(y, c), :]
        return remote(rows, rows, z_send.at[c], z_recv.at[c], peer)

    def to_both(c, dst):
        arrived(ybuf[c], y_recv.at[c])
        dst[own_rows(y, c), :] = ybuf[c][root_y]
        z_copy(c, dst, above).start()
        z_copy(c, dst, below).start()

    passes_up = (step == 1) & (near_top == 0)
    passes_down = (step == NZ - 1) & (near_top == 1)

    def onward(c, dst):
        rows = dst.at[own_rows(y, c), :]
        arrived(rows, z_recv.at[c])

        @pl.when(passes_up)
        def _():
            z_copy(c, dst, above).start()

        @pl.when(passes_down)
        def _():
            z_copy(c, dst, below).start()

    def spread(c, dst):
        rows = dst.at[own_rows(y, c), :]
        for peer in y_peers:
            remote(rows, rows, g_send.at[c], g_recv.at[c], peer).start()

    def from_root(parts, dst):
        @pl.when(step == 0)
        def _():
            for c in parts:
                to_both(c, dst)
                spread(c, dst)

    def from_z(c, dst):
        @pl.when(step != 0)
        def _():
            onward(c, dst)
            spread(c, dst)

    def three(sem):
        arrived(ybuf[0].at[pl.ds(0, NY - 1)], sem)

    first = list(range(HALVES))
    second = [HALVES + h for h in first]

    scatter(0, k_ref, kh, recv.at[0], (2, 3, 1, 0))
    scatter(1, v_ref, vh, recv.at[1], (2, 3, 1, 0))
    scatter(2, q_ref, qh, q_recv.at[zl], (0, 1, 2, 3))

    arrived(kh, recv.at[0])

    @pl.when(step == 0)
    def _():
        for c in first:
            y_start(c, kh)

    from_root(first, ak)
    arrived(vh, recv.at[1])

    @pl.when(step == 0)
    def _():
        for c in second:
            y_start(c, vh)

    def lane_of(i):
        low = lax.rem(i, 2)
        flip = zl + low - 2 * low * (zl % 2)
        return lax.rem(flip + 2 * lax.div(i, 2), NL)

    def local(i, carry):
        lane = lane_of(i)

        @pl.when(i == 0)
        def _():
            from_z(first[0], ak)

        @pl.when(i == 1)
        def _():
            from_root(second, av)
            from_z(first[1], ak)

        @pl.when(i == 2)
        def _():
            from_z(second[0], av)

        @pl.when(i == 3)
        def _():
            from_z(second[1], av)

        base = pl.multiple_of(lane * stretch, stretch)
        arrived(qh.at[pl.ds(base, stretch), :], q_recv.at[lane])

        def body(n, inner):
            local_block(
                pl.multiple_of(base + n * bq, bq),
                bq, length, qh, kh, vh, posc, posr, s_scr, acc_loc, m_loc, l_loc,
            )
            return inner

        lax.fori_loop(0, per_stretch, body, 0)
        return carry

    lax.fori_loop(0, NL, local, 0)
    for c in first:
        three(g_recv.at[c])

    def block_start(i):
        lane = lane_of(NL - 1 - lax.div(i, per_stretch))
        turn = lax.rem(i + lax.div(spot, per_block), per_stretch)
        return pl.multiple_of(lane * stretch + turn * bq, bq)

    def far_first(i, carry):
        far_chances(block_start(i), bq, length, qh, ak, s_scr, p_far, m_far)
        return carry

    lax.fori_loop(0, NL * per_stretch, far_first, 0)
    for c in second:
        three(g_recv.at[c])

    def far_second(i, carry):
        r0 = block_start(i)
        far_block(r0, bq, bias, av, p_far, m_far, acc_loc, m_loc, l_loc, oh)
        for n in range(per_block):
            peer = lax.div(r0, tokens) + n
            rows = pl.ds(pl.multiple_of(peer * tokens, tokens), tokens)
            src = oh.at[rows, :]
            dst = out_ref.at[0, :, my_columns]

            @pl.when(peer == me)
            def _():
                pltpu.make_async_copy(src, dst, recv.at[2]).start()

            @pl.when(peer != me)
            def _():
                remote(src, dst, send.at[3], recv.at[2], (grp, peer)).start()

        return carry

    lax.fori_loop(0, NL * per_stretch, far_second, 0)

    most = pl.ds(0, (shards - 1) * tokens)
    for i, buf in enumerate((kh, vh, qh, oh)):
        arrived(buf.at[most, :], send.at[i])
    for c in first + second:
        three(g_send.at[c])

    @pl.when(step == 0)
    def _():
        for c in first + second:
            three(y_send.at[c])
            arrived(ybuf[c].at[pl.ds(0, 2)], z_send.at[c])

    @pl.when(passes_up | passes_down)
    def _():
        for c in first + second:
            arrived(ybuf[c].at[0], z_send.at[c])

    arrived(out_ref, recv.at[2])


def solution(mesh):
    shards = mesh.shape["sp"]

    def attend_from(source, anchor, positions, queries, keys, values):
        tokens = queries.shape[1]
        length = tokens * shards
        bq = max(tokens, min(BQ, length // NL))
        part = length // NY // HALVES
        chunks = 2 * HALVES
        bf16 = jnp.bfloat16
        head = pltpu.VMEM((length, HD), bf16)
        wide = pltpu.VMEM((length, HD), jnp.float32)
        dma = pltpu.SemaphoreType.DMA
        vmem = pl.BlockSpec(memory_space=pltpu.VMEM)
        return pl.pallas_call(
            functools.partial(kernel, source, shards, length, tokens, bq),
            out_shape=jax.ShapeDtypeStruct(queries.shape, bf16),
            in_specs=[pl.BlockSpec(memory_space=pltpu.SMEM), vmem, vmem, vmem, vmem],
            out_specs=vmem,
            scratch_shapes=[
                head, head, head, head, head, head,
                wide,
                pltpu.VMEM((1, length), jnp.float32),
                pltpu.VMEM((bq, length), jnp.float32),
                pltpu.VMEM((length, length), bf16),
                wide, wide, wide, wide,
                [pltpu.VMEM((NY, part, HD), bf16)] * chunks,
                dma((4,)), dma((3,)), dma((NL,)),
                dma((chunks,)), dma((chunks,)),
                dma((chunks,)), dma((chunks,)),
                dma((chunks,)), dma((chunks,)),
            ],
            compiler_params=pltpu.CompilerParams(
                collective_id=source, has_side_effects=True
            ),
            name=f"star_attention_{source}",
        )(anchor, positions, queries, keys, values)

    def on_device(queries, keys, values, positions, anchor):
        source = anchor[0] & (NZ - 1)
        branches = [functools.partial(attend_from, n) for n in range(NZ)]
        return lax.switch(source, branches, anchor, positions, queries, keys, values)

    return jax.shard_map(
        on_device,
        mesh=mesh,
        in_specs=(
            P("grp", "sp", None),
            P("grp", "sp", None),
            P("grp", "sp", None),
            P("grp", None),
            P(),
        ),
        out_specs=P("grp", "sp", None),
        check_vma=False,
    )
```

time: 428 us -> 90.5 us (0.21)
  waiting for transfers between devices: 202 us -> 0 us
  other arithmetic: 93 us -> 0 us
  Pallas kernels: 0 us -> 84.3 us
  local copies, waits for them, and re-layouts: 46.2 us -> 1.49 us
  blocking collectives: 28.6 us -> 0 us
  starting transfers between devices: 27 us -> 0 us
  matrix products: 15.6 us -> 0 us
  between operations: 14.3 us -> 0.66 us
  loops' own time: 0.18 us -> 4.48 us
    psum x1 -> x0, waiting for transfers between devices: 202 us -> none  [broadcast(): return lax.psum(block, axis)]
    pallas_call x0 -> x1, Pallas kernels: none -> 84.3 us  [attend_from(): pl.pallas_call(functools.partial(kernel, source, shards, length, tokens,...]
    unnamed x5 -> x0, other arithmetic: 79 us -> none
    unnamed x21 -> x1, local copies, waits for them, and re-layouts: 31.8 us -> 0.8 us
    all_to_all x1 -> x0, blocking collectives: 28.6 us -> none  [on_device(): lax.all_to_all(attended_heads[None], 'sp', split_axis=1, concat_axis=2, t...]
    all_to_all x3 -> x0, starting transfers between devices: 26.7 us -> none  [the longest x1 11 us: on_device(): lax.all_to_all(keys, 'sp', split_axis=2, concat_axis=1, tiled=True)]
    dot_general x8 -> x0, matrix products: 15.6 us -> none  [the longest x4 10.6 us: one_block(): jnp.einsum('hqk,khd->qhd', probs, value_rows, preferred_element_type=jnp....]
    all_to_all x10 -> x0, local copies, waits for them, and re-layouts: 10.6 us -> none  [the longest x3 3.84 us: on_device(): lax.all_to_all(values, 'sp', split_axis=2, concat_axis=1, tiled=True)]
  transfers between devices with their start and end apart: 4 -> 0, of which waited for: 1 -> 0; matrix products, arithmetic and copies ran while one was open for 19% -> 0% of each run, Pallas kernels for 0% -> 0%
where the time goes in v2:
time: 90.5 us; the launch traced here: 90.9 us
  Pallas kernels  84.3 us (93%)
  loops' own time  4.48 us (5%)
  local copies, waits for them, and re-layouts  1.49 us (2%)
    pallas_call x1, Pallas kernels, attend_from(): pl.pallas_call(functools.partial(kernel, source, shards, length, tokens,...  84.3 us
    another operation x1, loops' own time, on_device(): lax.switch(source, branches, anchor, positions, queries, keys, values)  4.48 us

profile of v2, /device:TPU:1, one launch (start us, length us, event | category | flops | bytes accessed | tf_op | source)
XLA Modules:
  0.0 90.9 jit_solution(3483654161281019239)
XLA Ops:
  0.7 89.4 %conditional.1 = (bf16[1,64,4096]{2,1,0:T(8,128)(2,1)S(1)}) conditional(s32[]{:T(128)} %bitcast, (s32[1]{0:T(128)}, s32[1,2048]{1,0:T(1,128)}, bf16[1,64,4096]{2,1,0:T(8,128)(2,1)}, bf16[1,64,4096]{2,1,0:T(8,128)(2,1)}, bf16[1,64,4096]{2,1,0:T(8,128)(2,1)}) %tuple.17, (s32[1]{0:T(128)}, s32[1,2048]{1,0:T(1,128)}, ...), branch_computations={%region_0.0_spmd, %region_1.0_spmd, %region_2.0_spmd, %region_3.0_... | conditional | bytes 32804 | solution.py:401
  4.9 0.0 copy-start.3
  4.9 0.7 copy-done.3
  5.6 84.3 %star_attention_3.1 = bf16[1,64,4096]{2,1,0:T(8,128)(2,1)S(1)} custom-call(s32[1]{0:T(128)} %get-tuple-element.65.anchor_ref, s32[1,2048]{1,0:T(1,128)S(1)} %copy-done.3, bf16[1,64,4096]{2,1,0:T(8,128)(2,1)} %get-tuple-element.94.q_ref, bf16[1,64,4096]{2,1,0:T(8,128)(2,1)} %get-tuple-element.98.k_ref, bf16[1,64,4096]{2,1,0:T(8,128)(2,1)} %get-tuple-element.102.v_ref), custom_call_target="tpu_custom_call" | custom-call | tf_op jit(solution)/shard_map/cond/branch_3_fun/star_attention_3/pallas_call | solution.py:374
  90.1 0.8 copy.32
Async XLA Ops:
  4.9 0.7 copy-start.3

commit v3 on v2

--- a/solution.py
+++ b/solution.py
@@ -12,9 +12,13 @@
 NEG = -1e30
 NY = 4
 NZ = 4
-HALVES = 2
 NL = 4
 BQ = 512
+FIRST = (
+    (0, 0), (0, 1), (1, 0), (1, 1), (0, 2), (0, 3),
+    (1, 2), (1, 3), (2, 0), (2, 1),
+)
+LAST = ((2, 2), (2, 3))
 C = math.log2(math.e) / math.sqrt(HD)
 MESH = pl.DeviceIdType.MESH
 NT = (((1,), (1,)), ((), ()))
@@ -87,7 +91,7 @@
     anchor_ref, pos_ref, q_ref, k_ref, v_ref, out_ref,
     qh, kh, vh, ak, av, oh, posc, posr, s_scr, p_far, acc_loc, m_loc, l_loc, m_far,
     ybuf,
-    send, recv, q_recv, y_send, y_recv, z_send, z_recv, g_send, g_recv,
+    send, recv, lane_recv, y_send, y_recv, z_send, z_recv, g_send, g_recv,
 ):
     grp = lax.axis_index("grp")
     me = lax.axis_index("sp")
@@ -97,9 +101,8 @@
     zl = me // side
     spot = me % side
     step = (z + NZ - source) % NZ
-    quarter = length // NY
-    part = quarter // HALVES
     stretch = length // NL
+    part = stretch // NY
     per_stretch = stretch // bq
     per_block = bq // tokens
 
@@ -180,8 +183,10 @@
     def arrived(dst, sem):
         pltpu.make_async_copy(dst, dst, sem).wait()
 
+    root_zl = zl + (step % 2) * (NL - 1 - 2 * zl)
+
     def own_rows(j, c):
-        start = j * quarter + (c % HALVES) * part
+        start = turned(root_zl, c % NL) * stretch + j * part
         return pl.ds(pl.multiple_of(start, part), part)
 
     def y_start(c, src):
@@ -223,98 +228,125 @@
         for peer in y_peers:
             remote(rows, rows, g_send.at[c], g_recv.at[c], peer).start()
 
-    def from_root(parts, dst):
+    def three(sem):
+        arrived(ybuf[0].at[pl.ds(0, NY - 1)], sem)
+
+    keys = list(range(NL))
+    values = [NL + d for d in keys]
+
+    def scatter_all(plan):
+        tensors = ((k_ref, kh), (v_ref, vh), (q_ref, qh))
+        for i, d in plan:
+            src, dst = tensors[i]
+            scatter(i, src, dst, lane_recv.at[i, zl], (d,))
+
+    def stretch_in(c):
+        lane = turned(zl, c % NL)
+        buf = (kh, vh)[c // NL]
+        rows = pl.ds(pl.multiple_of(lane * stretch, stretch), stretch)
+        arrived(buf.at[rows, :], lane_recv.at[c // NL, lane])
+
         @pl.when(step == 0)
         def _():
+            y_start(c, buf)
+
+    def from_root(*parts):
+        @pl.when(step == 0)
+        def _():
             for c in parts:
+                dst = (ak, av)[c // NL]
                 to_both(c, dst)
                 spread(c, dst)
 
-    def from_z(c, dst):
+    def from_z(*parts):
         @pl.when(step != 0)
         def _():
-            onward(c, dst)
-            spread(c, dst)
-
-    def three(sem):
-        arrived(ybuf[0].at[pl.ds(0, NY - 1)], sem)
-
-    first = list(range(HALVES))
-    second = [HALVES + h for h in first]
-
-    scatter(0, k_ref, kh, recv.at[0], (2, 3, 1, 0))
-    scatter(1, v_ref, vh, recv.at[1], (2, 3, 1, 0))
-    scatter(2, q_ref, qh, q_recv.at[zl], (0, 1, 2, 3))
-
-    arrived(kh, recv.at[0])
+            for c in parts:
+                dst = (ak, av)[c // NL]
+                onward(c, dst)
+                spread(c, dst)
+
+    scatter_all(FIRST)
+    k0, k1, k2, k3 = keys
+    v0, v1, v2, v3 = values
+    stretch_in(k0)
+    stretch_in(k1)
+    stretch_in(v0)
+    from_root(k0)
+    stretch_in(v1)
+    from_root(k1, v0, v1)
+    from_z(k0, k1)
+    stretch_in(k2)
+    stretch_in(k3)
+
+    @pl.when(step != 0)
+    def _():
+        scatter_all(LAST)
+
+    from_root(k2, k3)
+    from_z(v0, v1, k2, k3)
+    stretch_in(v2)
+    stretch_in(v3)
+    from_root(v2, v3)
 
     @pl.when(step == 0)
     def _():
-        for c in first:
-            y_start(c, kh)
-
-    from_root(first, ak)
-    arrived(vh, recv.at[1])
-
-    @pl.when(step == 0)
-    def _():
-        for c in second:
-            y_start(c, vh)
+        scatter_all(LAST)
 
     def lane_of(i):
         low = lax.rem(i, 2)
         flip = zl + low - 2 * low * (zl % 2)
         return lax.rem(flip + 2 * lax.div(i, 2), NL)
 
-    def local(i, carry):
+    def middle(n, carry):
+        is_local = (n < 3) | (n == 6)
+        i = jnp.where(n < 3, n, jnp.where(n < 6, n - 3, 3))
         lane = lane_of(i)
-
-        @pl.when(i == 0)
-        def _():
-            from_z(first[0], ak)
-
-        @pl.when(i == 1)
-        def _():
-            from_root(second, av)
-            from_z(first[1], ak)
-
-        @pl.when(i == 2)
-        def _():
-            from_z(second[0], av)
-
-        @pl.when(i == 3)
-        def _():
-            from_z(second[1], av)
-
         base = pl.multiple_of(lane * stretch, stretch)
-        arrived(qh.at[pl.ds(base, stretch), :], q_recv.at[lane])
-
-        def body(n, inner):
-            local_block(
-                pl.multiple_of(base + n * bq, bq),
-                bq, length, qh, kh, vh, posc, posr, s_scr, acc_loc, m_loc, l_loc,
-            )
-            return inner
-
-        lax.fori_loop(0, per_stretch, body, 0)
+
+        @pl.when(n == 2)
+        def _():
+            from_z(v2)
+
+        @pl.when(n == 3)
+        def _():
+            from_z(v3)
+            for c in keys:
+                three(g_recv.at[c])
+
+        @pl.when(is_local)
+        def _():
+            arrived(qh.at[pl.ds(base, stretch), :], lane_recv.at[2, lane])
+
+            def body(m, inner):
+                local_block(
+                    pl.multiple_of(base + m * bq, bq),
+                    bq, length, qh, kh, vh, posc, posr, s_scr, acc_loc, m_loc, l_loc,
+                )
+                return inner
+
+            lax.fori_loop(0, per_stretch, body, 0)
+
+        @pl.when(jnp.logical_not(is_local))
+        def _():
+            def body(m, inner):
+                far_chances(
+                    pl.multiple_of(base + m * bq, bq), bq, length, qh, ak, s_scr, p_far, m_far
+                )
+                return inner
+
+            lax.fori_loop(0, per_stretch, body, 0)
+
         return carry
 
-    lax.fori_loop(0, NL, local, 0)
-    for c in first:
+    lax.fori_loop(0, 2 * NL, middle, 0)
+    for c in values:
         three(g_recv.at[c])
 
     def block_start(i):
         lane = lane_of(NL - 1 - lax.div(i, per_stretch))
         turn = lax.rem(i + lax.div(spot, per_block), per_stretch)
         return pl.multiple_of(lane * stretch + turn * bq, bq)
-
-    def far_first(i, carry):
-        far_chances(block_start(i), bq, length, qh, ak, s_scr, p_far, m_far)
-        return carry
-
-    lax.fori_loop(0, NL * per_stretch, far_first, 0)
-    for c in second:
-        three(g_recv.at[c])
 
     def far_second(i, carry):
         r0 = block_start(i)
@@ -340,18 +372,18 @@
     most = pl.ds(0, (shards - 1) * tokens)
     for i, buf in enumerate((kh, vh, qh, oh)):
         arrived(buf.at[most, :], send.at[i])
-    for c in first + second:
+    for c in keys + values:
         three(g_send.at[c])
 
     @pl.when(step == 0)
     def _():
-        for c in first + second:
+        for c in keys + values:
             three(y_send.at[c])
             arrived(ybuf[c].at[pl.ds(0, 2)], z_send.at[c])
 
     @pl.when(passes_up | passes_down)
     def _():
-        for c in first + second:
+        for c in keys + values:
             arrived(ybuf[c].at[0], z_send.at[c])
 
     arrived(out_ref, recv.at[2])
@@ -364,8 +396,8 @@
         tokens = queries.shape[1]
         length = tokens * shards
         bq = max(tokens, min(BQ, length // NL))
-        part = length // NY // HALVES
-        chunks = 2 * HALVES
+        part = length // NL // NY
+        chunks = 2 * NL
         bf16 = jnp.bfloat16
         head = pltpu.VMEM((length, HD), bf16)
         wide = pltpu.VMEM((length, HD), jnp.float32)
@@ -384,7 +416,7 @@
                 pltpu.VMEM((length, length), bf16),
                 wide, wide, wide, wide,
                 [pltpu.VMEM((NY, part, HD), bf16)] * chunks,
-                dma((4,)), dma((3,)), dma((NL,)),
+                dma((4,)), dma((3,)), dma((3, NL)),
                 dma((chunks,)), dma((chunks,)),
                 dma((chunks,)), dma((chunks,)),
                 dma((chunks,)), dma((chunks,)),

time: 90.5 us -> 85.7 us (0.947)
  loops' own time: 4.48 us -> 0.26 us
    another operation x1, loops' own time: 4.48 us -> 0.26 us  [on_device(): lax.switch(source, branches, anchor, positions, queries, keys, values)]
where the time goes in v3:
time: 85.7 us; the launch traced here: 86 us
  Pallas kernels  83.6 us (98%)
  local copies, waits for them, and re-layouts  1.49 us (2%)
    pallas_call x1, Pallas kernels, attend_from(): pl.pallas_call(functools.partial(kernel, source, shards, length, tokens,...  83.6 us

profile of v3, /device:TPU:1, one launch (start us, length us, event | category | flops | bytes accessed | tf_op | source)
XLA Modules:
  0.0 86.0 jit_solution(7431375641518452708)
XLA Ops:
  0.7 84.5 %conditional.1 = (bf16[1,64,4096]{2,1,0:T(8,128)(2,1)S(1)}) conditional(s32[]{:T(128)} %bitcast, (s32[1]{0:T(128)}, s32[1,2048]{1,0:T(1,128)}, bf16[1,64,4096]{2,1,0:T(8,128)(2,1)}, bf16[1,64,4096]{2,1,0:T(8,128)(2,1)}, bf16[1,64,4096]{2,1,0:T(8,128)(2,1)}) %tuple.17, (s32[1]{0:T(128)}, s32[1,2048]{1,0:T(1,128)}, ...), branch_computations={%region_0.0_spmd, %region_1.0_spmd, %region_2.0_spmd, %region_3.0_... | conditional | bytes 32804 | solution.py:433
  0.7 0.0 copy-start.1
  0.7 0.7 copy-done.1
  1.4 83.6 %star_attention_1.1 = bf16[1,64,4096]{2,1,0:T(8,128)(2,1)S(1)} custom-call(s32[1]{0:T(128)} %get-tuple-element.55.anchor_ref, s32[1,2048]{1,0:T(1,128)S(1)} %copy-done.1, bf16[1,64,4096]{2,1,0:T(8,128)(2,1)} %get-tuple-element.92.q_ref, bf16[1,64,4096]{2,1,0:T(8,128)(2,1)} %get-tuple-element.96.k_ref, bf16[1,64,4096]{2,1,0:T(8,128)(2,1)} %get-tuple-element.100.v_ref), custom_call_target="tpu_custom_call" | custom-call | tf_op jit(solution)/shard_map/cond/branch_1_fun/star_attention_1/pallas_call | solution.py:406
  85.2 0.8 copy.32
Async XLA Ops:
  0.7 0.7 copy-start.1
